TPU v7x, 256 devices: a whole 4x4x8 slice. The times are simulated.
256 devices in a mesh: expert: 64 (over x, z, core), dp: 4 (over y).
Axes of the slice: x: 4, y: 4, z: 8, core: 2. Of those that a mesh axis runs over, the one named last changes fastest.
Arguments:
- tokens: bfloat16 [8192, 3584], P('expert', 'dp'), may hold values from -6 to 6
- cotangent: bfloat16 [8192, 3584], P('expert', 'dp'), may hold values from -6 to 6
- expert_ids: int32 [8192, 8], P('expert'), may hold values from 0 to 63, all different within a row; in each aligned block of 128 rows (0 to 127, 128 to 255, ...) at most 18 rows name the same one
- gate_units: int32 [8192, 8], P('expert'), may hold values from 1 to 255
- w_in: bfloat16 [64, 3584, 1024], P('expert', 'dp'), may hold values from -0.09375 to 0.09375
- w_out: bfloat16 [64, 1024, 3584], P('expert', None, 'dp'), may hold values from -0.1875 to 0.1875
- shared_in: bfloat16 [3584, 1024], P('dp', 'expert'), may hold values from -0.09375 to 0.09375
- shared_out: bfloat16 [1024, 3584], P('expert', 'dp'), may hold values from -0.1875 to 0.1875
Outputs:
- mixed_out: bfloat16 [8192, 3584], P('expert', 'dp')
- input_grad: bfloat16 [8192, 3584], P('expert', 'dp')
- grad_w_in: bfloat16 [64, 3584, 1024], P('expert', 'dp')
- grad_w_out: bfloat16 [64, 1024, 3584], P('expert', None, 'dp')
- grad_shared_in: bfloat16 [3584, 1024], P('dp', 'expert')
- grad_shared_out: bfloat16 [1024, 3584], P('expert', 'dp')
Inputs may be any that keep to these rules, and one draw needn't show every extreme that they name: `expert_ids`: each row names 8 different experts. In each aligned block of 128 rows (the tokens of one index of expert) no expert is named by more than 18 rows, a bound that some block reaches.
All inputs are finite; a program needn't handle non-finite values.
Results may differ from a plain program's by a relative error of at most 0.02.
Values may be sent and summed in bfloat16 or wider, within the bound.
No kernel may reach another device: no remote copies, remote signals or barrier semaphores. Data moves between devices by JAX's collectives and lax.ppermute only.
A program may use at most 128 MiB of HBM per device.

v0:
```python
import jax
import jax.numpy as jnp
from jax import lax
from jax.sharding import PartitionSpec as P


def silu_slope(inputs):
    logistic = jax.nn.sigmoid(inputs)
    return logistic * (1.0 + inputs * (1.0 - logistic))


def contract(first_op, second_op, first_axis, second_axis):
    return lax.dot_general(
        first_op,
        second_op,
        (((first_axis,), (second_axis,)), ((), ())),
        preferred_element_type=jnp.float32,
    )


def local(tokens, cotangent, expert_ids, gate_units, w_in, w_out, shared_in, shared_out):
    experts = lax.axis_size("expert")
    tok_rows, features = tokens.shape
    per_token = expert_ids.shape[1]
    capacity = min(tok_rows, tok_rows * per_token // experts + tok_rows // 64)
    slot_count = experts * capacity
    pair_count = tok_rows * per_token
    flat_ids = expert_ids.reshape(pair_count)
    weights = gate_units.reshape(pair_count).astype(jnp.float32) / 256.0
    one_hot = (flat_ids[:, None] == jnp.arange(experts, dtype=jnp.int32)[None, :]).astype(jnp.int32)
    slot_rank = jnp.sum((jnp.cumsum(one_hot, axis=0) - 1) * one_hot, axis=1)
    target = flat_ids * capacity + slot_rank
    pair_of_slot = (
        jnp.zeros((slot_count,), jnp.int32).at[target].set(jnp.arange(pair_count, dtype=jnp.int32))
    )
    filled = jnp.zeros((slot_count,), jnp.bool_).at[target].set(True)
    token_of_slot = pair_of_slot // per_token
    outgoing = jnp.where(filled[:, None], tokens[token_of_slot], jnp.zeros((), jnp.bfloat16))
    arrived = lax.all_to_all(
        outgoing.reshape(experts, capacity, features),
        "expert",
        split_axis=0,
        concat_axis=0,
        tiled=True,
    ).reshape(slot_count, features)
    full_in, full_out = (
        lax.all_gather(shared_in, "expert", axis=1, tiled=True),
        lax.all_gather(shared_out, "expert", axis=0, tiled=True),
    )
    routed_part = jnp.dot(arrived, w_in[0], preferred_element_type=jnp.float32)
    shared_part = jnp.dot(tokens, full_in, preferred_element_type=jnp.float32)
    pre_act, shared_pre = (
        lax.psum(routed_part.astype(jnp.bfloat16), "dp").astype(jnp.float32),
        lax.psum(shared_part.astype(jnp.bfloat16), "dp").astype(jnp.float32),
    )
    hidden = jax.nn.silu(pre_act).astype(jnp.bfloat16)
    shared_hidden = jax.nn.silu(shared_pre).astype(jnp.bfloat16)
    expert_out = jnp.dot(hidden, w_out[0], preferred_element_type=jnp.float32).astype(jnp.bfloat16)
    returned = lax.all_to_all(
        expert_out.reshape(experts, capacity, features),
        "expert",
        split_axis=0,
        concat_axis=0,
        tiled=True,
    ).reshape(slot_count, features)
    picked = returned[target].astype(jnp.float32) * weights[:, None]
    routed_sum = jnp.sum(picked.reshape(tok_rows, per_token, features), axis=1)
    mixed_out = (
        jnp.dot(shared_hidden, full_out, preferred_element_type=jnp.float32) + routed_sum
    ).astype(jnp.bfloat16)
    scaled = weights[pair_of_slot][:, None] * cotangent[token_of_slot].astype(jnp.float32)
    grad_out = jnp.where(filled[:, None], scaled, jnp.float32(0.0)).astype(jnp.bfloat16)
    grad_rows = lax.all_to_all(
        grad_out.reshape(experts, capacity, features),
        "expert",
        split_axis=0,
        concat_axis=0,
        tiled=True,
    ).reshape(slot_count, features)
    routed_back = contract(grad_rows, w_out[0], 1, 1)
    shared_back = contract(cotangent, full_out, 1, 1)
    hidden_grad, shared_hgrad = (
        lax.psum(routed_back.astype(jnp.bfloat16), "dp").astype(jnp.float32),
        lax.psum(shared_back.astype(jnp.bfloat16), "dp").astype(jnp.float32),
    )
    pre_grad = (hidden_grad * silu_slope(pre_act)).astype(jnp.bfloat16)
    shared_pgrad = (shared_hgrad * silu_slope(shared_pre)).astype(jnp.bfloat16)
    input_rows = contract(pre_grad, w_in[0], 1, 1).astype(jnp.bfloat16)
    sent_back = lax.all_to_all(
        input_rows.reshape(experts, capacity, features),
        "expert",
        split_axis=0,
        concat_axis=0,
        tiled=True,
    ).reshape(slot_count, features)
    routed_dx = jnp.sum(
        sent_back[target].astype(jnp.float32).reshape(tok_rows, per_token, features), axis=1
    )
    input_grad = (contract(shared_pgrad, full_in, 1, 1) + routed_dx).astype(jnp.bfloat16)
    grad_w_in = contract(arrived, pre_grad, 0, 0).astype(jnp.bfloat16)[None]
    grad_w_out = contract(hidden, grad_rows, 0, 0).astype(jnp.bfloat16)[None]
    partial_in = contract(tokens, shared_pgrad, 0, 0)
    partial_out = contract(shared_hidden, cotangent, 0, 0)
    summed_in, summed_out = (
        lax.psum_scatter(partial_in, "expert", scatter_dimension=1, tiled=True),
        lax.psum_scatter(partial_out, "expert", scatter_dimension=0, tiled=True),
    )
    return (
        mixed_out,
        input_grad,
        grad_w_in,
        grad_w_out,
        summed_in.astype(jnp.bfloat16),
        summed_out.astype(jnp.bfloat16),
    )


def solution(mesh):
    return jax.shard_map(
        local,
        mesh=mesh,
        in_specs=(
            P("expert", "dp"),
            P("expert", "dp"),
            P("expert", None),
            P("expert", None),
            P("expert", "dp", None),
            P("expert", None, "dp"),
            P("dp", "expert"),
            P("expert", "dp"),
        ),
        out_specs=(
            P("expert", "dp"),
            P("expert", "dp"),
            P("expert", "dp", None),
            P("expert", None, "dp"),
            P("dp", "expert"),
            P("expert", "dp"),
        ),
        check_vma=False,
    )
```

profile of v0, /device:TPU:8, one launch (start us, length us, event | category | flops | bytes accessed | tf_op | source)
XLA Modules:
  0.0 643.2 jit_solution(7571708094391485513)
XLA Ops:
  7.2 0.7 all-gather.5.cloned.1.call-update
  7.9 0.7 broadcast_multiply_fusion
  8.6 0.8 copy.16
  9.4 0.1 eq.29
  9.6 0.1 copy.15
  9.7 0.1 mul.68
  9.8 18.0 %reduce-window.6 = s32[64,8,128]{2,1,0:T(8,128)S(1)} reduce-window(s32[64,8,128]{2,1,0:T(8,128)S(1)} %fusion.25, s32[]{:T(128)} %constant.19.clone.1), window={size=1x1x128 pad=0_0x0_0x127_0}, to_apply=%region_1.2 | reduce-window | flops 8323072 | bytes 524292 | tf_op jit(solution)/shard_map/reduce-window
  27.8 0.1 slice.18
  28.0 0.1 copy.18
  28.2 0.1 add_add_fusion
  28.5 4.3 scatter_custom_fusion.1
  32.8 4.3 scatter_custom_fusion
  37.2 0.1 broadcast_in_dim.54
  37.4 4.9 gather_fusion
  42.3 4.1 gather.18
  46.4 3.8 broadcast_select_fusion
  50.3 12.3 %all-to-all-start = ((bf16[64,18,896]{2,1,0:T(8,128)(2,1)}), bf16[64,18,896]{2,1,0:T(8,128)(2,1)}, u32[]{:S(2)}, u32[]{:S(2)}) async-start(bf16[64,18,896]{2,1,0:T(8,128)(2,1)} %broadcast_select_fusion), calls=%async_computation | async-start | bytes 5505024 | tf_op jit(solution)/shard_map/all_to_all | solution.py:39
  62.6 0.7 all-gather.3.cloned.1.call-update
  63.3 0.1 copy.20
  63.4 0.1 div.38
  63.5 4.6 gather_fusion.2
  68.1 0.1 mul.76
  68.3 4.9 gather_fusion.3
  73.2 4.6 reshape.130
  77.8 4.1 select_convert_fusion
  81.8 50.9 %all-to-all-done = bf16[64,18,896]{2,1,0:T(8,128)(2,1)} async-done(((bf16[64,18,896]{2,1,0:T(8,128)(2,1)}), bf16[64,18,896]{2,1,0:T(8,128)(2,1)}, u32[]{:S(2)}, u32[]{:S(2)}) %all-to-all-start) | async-done | bytes 2064416 | tf_op jit(solution)/shard_map/all_to_all | solution.py:39
  132.8 5.7 all-to-all-start.2
  138.5 0.2 all-reduce.3.cloned.1.call-start
  138.8 2.9 convolution_convert_fusion.4
  141.7 39.4 %all-gather.3.cloned.1.call-done = bf16[896,1024]{0,1:T(8,128)(2,1)} async-done(((bf16[896,16]{0,1:T(8,128)(2,1)}), bf16[896,1024]{0,1:T(8,128)(2,1)}) %all-gather.3.cloned.1.call-update) | async-done | bytes 1835024 | tf_op jit(solution)/shard_map/all_gather | solution.py:47
  181.1 2.9 convolution_convert_fusion.5
  184.0 4.2 reshape.123
  188.2 5.5 convolution_convert_fusion.1
  193.6 13.7 %all-to-all-done.2 = bf16[64,18,896]{2,1,0:T(8,128)(2,1)} async-done(((bf16[64,18,896]{2,1,0:T(8,128)(2,1)}), bf16[64,18,896]{2,1,0:T(8,128)(2,1)}, u32[]{:S(2)}, u32[]{:S(2)}) %all-to-all-start.2) | async-done | bytes 2064416 | tf_op jit(solution)/shard_map/all_to_all | solution.py:73
  207.4 4.1 reshape.126
  211.5 6.2 convolution_convert_fusion
  217.8 111.4 %all-reduce.3.cloned.1.call-done = (bf16[1152,1024]{1,0:T(8,128)(2,1)}, bf16[128,1024]{1,0:T(8,128)(2,1)}, bf16[1152,1024]{1,0:T(8,128)(2,1)}, bf16[128,1024]{1,0:T(8,128)(2,1)}) async-done(((bf16[1152,1024]{1,0:T(8,128)(2,1)}, bf16[128,1024]{1,0:T(8,128)(2,1)}, bf16[1152,1024]{1,0:T(8,128)(2,1)}, bf16[128,1024]{1,0:T(8,128)(2,1)}), (bf16[1152,1024]{1,0:T(8,128)(2,1)}, bf16[128,1024]{1,0:T(8,128)(2,1)}, ...) | async-done | bytes 5242896 | tf_op jit(solution)/shard_map/psum | solution.py:53
  329.2 3.6 convolution_bitcast_fusion
  332.8 4.3 fusion.7
  337.1 1.4 copy-done.6
  338.5 3.8 convolution_convert_fusion.2
  342.3 4.2 reshape.127
  346.5 10.8 %all-to-all-start.3 = ((bf16[64,18,896]{2,1,0:T(8,128)(2,1)}), bf16[64,18,896]{2,1,0:T(8,128)(2,1)}, u32[]{:S(2)}, u32[]{:S(2)}) async-start(bf16[64,18,896]{2,1,0:T(8,128)(2,1)} %reshape.127), calls=%async_computation.3 | async-start | bytes 5505024 | tf_op jit(solution)/shard_map/all_to_all | solution.py:89
  357.3 0.3 reduce-scatter.5.cloned.1.call-start
  357.6 2.5 fusion.32
  360.2 5.0 convolution_convert_fusion.3
  365.1 2.3 reshape.124
  367.5 56.1 %all-to-all-done.3 = bf16[64,18,896]{2,1,0:T(8,128)(2,1)} async-done(((bf16[64,18,896]{2,1,0:T(8,128)(2,1)}), bf16[64,18,896]{2,1,0:T(8,128)(2,1)}, u32[]{:S(2)}, u32[]{:S(2)}) %all-to-all-start.3) | async-done | bytes 2064416 | tf_op jit(solution)/shard_map/all_to_all | solution.py:89
  423.6 7.0 %all-to-all-start.1 = ((bf16[64,18,896]{2,1,0:T(8,128)(2,1)}), bf16[64,18,896]{2,1,0:T(8,128)(2,1)}, u32[]{:S(2)}, u32[]{:S(2)}) async-start(bf16[64,18,896]{2,1,0:T(8,128)(2,1)} %reshape.124), calls=%async_computation.1 | async-start | bytes 5505024 | tf_op jit(solution)/shard_map/all_to_all | solution.py:59
  430.6 5.6 convert_bitcast_fusion.1
  436.3 4.1 convert_bitcast_fusion
  440.4 2.8 reshape.128
  443.2 5.3 gather_fusion.4
  448.5 51.4 %all-to-all-done.1 = bf16[64,18,896]{2,1,0:T(8,128)(2,1)} async-done(((bf16[64,18,896]{2,1,0:T(8,128)(2,1)}), bf16[64,18,896]{2,1,0:T(8,128)(2,1)}, u32[]{:S(2)}, u32[]{:S(2)}) %all-to-all-start.1) | async-done | bytes 2064416 | tf_op jit(solution)/shard_map/all_to_all | solution.py:59
  499.9 2.8 reshape.125
  502.7 5.3 gather_fusion.1
  508.0 2.9 convert_reduce_fusion
  510.9 1.2 fusion.8
  512.1 1.2 fusion.13
  513.3 0.4 copy-done.10
  513.7 1.2 fusion.14
  514.9 1.4 convert_element_type.125
  516.3 118.8 %reduce-scatter.5.cloned.1.call-done = f32[16,896]{1,0:T(8,128)} async-done(((f32[1024,896]{1,0:T(8,128)}), f32[16,896]{1,0:T(8,128)}) %reduce-scatter.5.cloned.1.call-update) | async-done | bytes 57360 | tf_op jit(solution)/shard_map/reduce_scatter | solution.py:106
  635.2 1.4 convert_element_type.126
  (47 shorter events, 0.6 us)
Async XLA Ops:
  7.2 181.0 %copy-start = (bf16[1,896,1024]{2,1,0:T(8,128)(2,1)S(1)}, bf16[1,896,1024]{2,1,0:T(8,128)(2,1)}, u32[]{:S(2)}) copy-start(bf16[1,896,1024]{2,1,0:T(8,128)(2,1)} %param.12) | copy-start | bytes 5505028
  7.2 30.2 %copy-start.2 = (bf16[128,896]{1,0:T(8,128)(2,1)S(1)}, bf16[128,896]{1,0:T(8,128)(2,1)}, u32[]{:S(2)}) copy-start(bf16[128,896]{1,0:T(8,128)(2,1)} %param.8) | copy-start | bytes 688132
  7.2 131.6 %all-gather.5.cloned.1.call-start = ((), (), s32[]{:S(2)}) async-start(), calls=%async_computation.7 | async-start | bytes 1863680 | tf_op jit(solution)/shard_map/all_gather | solution.py:48
  50.3 13.1 %copy-start.13 = (s32[128,8]{0,1:T(8,128)S(1)}, s32[128,8]{0,1:T(8,128)}, u32[]{:S(2)}) copy-start(s32[128,8]{0,1:T(8,128)} %param.11) | copy-start | bytes 12292
  50.3 82.5 %all-to-all-start = ((bf16[64,18,896]{2,1,0:T(8,128)(2,1)}), bf16[64,18,896]{2,1,0:T(8,128)(2,1)}, u32[]{:S(2)}, u32[]{:S(2)}) async-start(bf16[64,18,896]{2,1,0:T(8,128)(2,1)} %broadcast_select_fusion), calls=%async_computation | async-start | bytes 5505024 | tf_op jit(solution)/shard_map/all_to_all | solution.py:39
  62.6 118.5 %all-gather.3.cloned.1.call-start = ((), (), s32[]{:S(2)}) async-start(), calls=%async_computation.6 | async-start | bytes 1863680 | tf_op jit(solution)/shard_map/all_gather | solution.py:47
  63.5 4.7 copy-start.3
  132.8 74.6 %all-to-all-start.2 = ((bf16[64,18,896]{2,1,0:T(8,128)(2,1)}), bf16[64,18,896]{2,1,0:T(8,128)(2,1)}, u32[]{:S(2)}, u32[]{:S(2)}) async-start(bf16[64,18,896]{2,1,0:T(8,128)(2,1)} %select_convert_fusion), calls=%async_computation.2 | async-start | bytes 5505024 | tf_op jit(solution)/shard_map/all_to_all | solution.py:73
  138.5 190.7 %all-reduce.3.cloned.1.call-start = ((), (), s32[]{:S(2)}) async-start(), calls=%async_computation.10 | async-start | bytes 10485760 | tf_op jit(solution)/shard_map/psum | solution.py:53
  217.7 297.2 %reduce-scatter.3.cloned.1.call-start = ((), (), s32[]{:S(2)}) async-start(), calls=%async_computation.8 | async-start | bytes 3727360 | tf_op jit(solution)/shard_map/reduce_scatter | solution.py:105
  337.1 1.4 copy-start.6
  346.5 11.1 %copy-start.11 = (bf16[128,1024]{1,0:T(8,128)(2,1)S(1)}, bf16[128,1024]{1,0:T(8,128)(2,1)}, u32[]{:S(2)}) copy-start(bf16[128,1024]{1,0:T(8,128)(2,1)} %get-tuple-element.7) | copy-start | bytes 786436
  346.5 77.0 %all-to-all-start.3 = ((bf16[64,18,896]{2,1,0:T(8,128)(2,1)}), bf16[64,18,896]{2,1,0:T(8,128)(2,1)}, u32[]{:S(2)}, u32[]{:S(2)}) async-start(bf16[64,18,896]{2,1,0:T(8,128)(2,1)} %reshape.127), calls=%async_computation.3 | async-start | bytes 5505024 | tf_op jit(solution)/shard_map/all_to_all | solution.py:89
  357.3 277.8 %reduce-scatter.5.cloned.1.call-start = ((), (), s32[]{:S(2)}) async-start(), calls=%async_computation.9 | async-start | bytes 3727360 | tf_op jit(solution)/shard_map/reduce_scatter | solution.py:106
  367.5 63.1 %copy-start.7 = (bf16[1152,896]{1,0:T(8,128)(2,1)S(1)}, bf16[1152,896]{1,0:T(8,128)(2,1)}, u32[]{:S(2)}) copy-start(bf16[1152,896]{1,0:T(8,128)(2,1)} %reshape.123) | copy-start | bytes 6193156
  423.6 76.3 %all-to-all-start.1 = ((bf16[64,18,896]{2,1,0:T(8,128)(2,1)}), bf16[64,18,896]{2,1,0:T(8,128)(2,1)}, u32[]{:S(2)}, u32[]{:S(2)}) async-start(bf16[64,18,896]{2,1,0:T(8,128)(2,1)} %reshape.124), calls=%async_computation.1 | async-start | bytes 5505024 | tf_op jit(solution)/shard_map/all_to_all | solution.py:59
  430.6 5.7 copy-start.5
  430.6 5.6 copy-start.8
  508.0 2.9 copy-start.4
  508.0 4.1 copy-start.9
  512.1 1.6 copy-start.10
  512.1 1.6 copy-start.12
  512.1 124.5 %copy-start.1 = (bf16[1,896,1024]{2,1,0:T(8,128)(2,1)S(1)}, bf16[1,896,1024]{2,1,0:T(8,128)(2,1)}, u32[]{:S(2)}) copy-start(bf16[1,896,1024]{2,1,0:T(8,128)(2,1)} %param.12) | copy-start | bytes 5505028
Sparse Core Ops, SparseCore 0:
  10.7 85.2 all-gather.4
  98.7 82.3 all-gather.2
  217.8 111.2 all-reduce.2
  333.2 155.8 reduce-scatter.2
  493.6 141.5 reduce-scatter.4
where the time goes:
time: 644 us; the launch traced here: 643 us
  waiting for transfers between devices  443 us (69%)
  local copies, waits for them, and re-layouts  66.7 us (10%)
  matrix products  44.5 us (7%)
  other arithmetic  38.1 us (6%)
  starting transfers between devices  36.4 us (6%)
  between operations  14.1 us (2%)
    reduce_scatter x1, waiting for transfers between devices, local(): lax.psum_scatter(partial_out, 'expert', scatter_dimension=0, tiled=True)  119 us
    psum x1, waiting for transfers between devices, local(): lax.psum(routed_part.astype(jnp.bfloat16), 'dp').astype(jnp.float32)  111 us
    all_to_all x1, waiting for transfers between devices, local(): lax.all_to_all(input_rows.reshape(experts, capacity, features), 'expert',...  56.1 us
    all_to_all x1, waiting for transfers between devices, local(): lax.all_to_all(expert_out.reshape(experts, capacity, features), 'expert',...  51.4 us
    all_to_all x1, waiting for transfers between devices, local(): lax.all_to_all(outgoing.reshape(experts, capacity, features), 'expert', s...  50.9 us
    all_gather x1, waiting for transfers between devices, local(): lax.all_gather(shared_in, 'expert', axis=1, tiled=True)  39.4 us
    dot_general x8, matrix products, contract(): lax.dot_general(first_op, second_op, (((first_axis,), (second_axis,)), ((...  30 us
    another operation x2, other arithmetic  18 us
  transfers between devices with their start and end apart: 9, of which 7 were waited for; matrix products, arithmetic and copies ran while one was open for 21% of the time, Pallas kernels for 0%

commit v1 on v0

--- a/solution.py
+++ b/solution.py
@@ -44,7 +44,9 @@
         tiled=True,
     ).reshape(slot_count, features)
     full_in, full_out = (
-        lax.all_gather(shared_in, "expert", axis=1, tiled=True),
+        jnp.concatenate(
+            lax.all_to_all(jnp.stack([shared_in] * lax.axis_size("expert")), "expert", 0, 0), axis=1
+        ),
         lax.all_gather(shared_out, "expert", axis=0, tiled=True),
     )
     routed_part = jnp.dot(arrived, w_in[0], preferred_element_type=jnp.float32)

time: 644 us -> 652 us (1.012)
  starting transfers between devices: 36.4 us -> 44.1 us
    all_gather x1 -> x0, waiting for transfers between devices: 39.4 us -> none  [local(): lax.all_gather(shared_in, 'expert', axis=1, tiled=True)]
    all_to_all x1, waiting for transfers between devices: 13.7 us -> 35.5 us  [local(): lax.all_to_all(grad_out.reshape(experts, capacity, features), 'expert', s...]
    all_gather x1, waiting for transfers between devices: 0.02 us -> 14.7 us  [local(): lax.all_gather(shared_out, 'expert', axis=0, tiled=True)]
    all_to_all x0 -> x1, starting transfers between devices: none -> 12.2 us  [local(): lax.all_to_all(jnp.stack([shared_in] * lax.axis_size('expert')), 'expert'...]
  transfers between devices with their start and end apart: 9 -> 9, of which waited for: 7 -> 8; matrix products, arithmetic and copies ran while one was open for 21% -> 20% of each run, Pallas kernels for 0% -> 0%
where the time goes in v1:
time: 652 us; the launch traced here: 651 us
  waiting for transfers between devices  441 us (68%)
  local copies, waits for them, and re-layouts  67.9 us (10%)
  matrix products  46.1 us (7%)
  starting transfers between devices  44.1 us (7%)
  other arithmetic  37.4 us (6%)
  between operations  14.1 us (2%)
    reduce_scatter x1, waiting for transfers between devices, local(): lax.psum_scatter(partial_out, 'expert', scatter_dimension=0, tiled=True)  120 us
    psum x1, waiting for transfers between devices, local(): lax.psum(routed_part.astype(jnp.bfloat16), 'dp').astype(jnp.float32)  112 us
    all_to_all x1, waiting for transfers between devices, local(): lax.all_to_all(input_rows.reshape(experts, capacity, features), 'expert',...  56.1 us
    all_to_all x1, waiting for transfers between devices, local(): lax.all_to_all(expert_out.reshape(experts, capacity, features), 'expert',...  51.3 us
    all_to_all x1, waiting for transfers between devices, local(): lax.all_to_all(outgoing.reshape(experts, capacity, features), 'expert', s...  46.4 us
    all_to_all x1, waiting for transfers between devices, local(): lax.all_to_all(grad_out.reshape(experts, capacity, features), 'expert', s...  35.5 us
    dot_general x8, matrix products, contract(): lax.dot_general(first_op, second_op, (((first_axis,), (second_axis,)), ((...  31.6 us
    another operation x2, other arithmetic  18 us
  transfers between devices with their start and end apart: 9, of which 8 were waited for; matrix products, arithmetic and copies ran while one was open for 20% of the time, Pallas kernels for 0%

profile of v1, /device:TPU:8, one launch (start us, length us, event | category | flops | bytes accessed | tf_op | source)
XLA Modules:
  0.0 650.9 jit_solution(14599250163393378596)
XLA Ops:
  7.2 2.2 stack.2
  9.4 12.2 %all-to-all-start = ((bf16[64,896,16]{1,2,0:T(8,128)(2,1)}), bf16[64,896,16]{1,2,0:T(8,128)(2,1)}, u32[]{:S(2)}, u32[]{:S(2)}) async-start(bf16[64,896,16]{1,2,0:T(8,128)(2,1)} %stack.2), calls=%async_computation | async-start | bytes 3670016 | tf_op jit(solution)/shard_map/all_to_all | solution.py:48
  21.6 0.1 copy.17
  21.7 0.1 eq.29
  21.8 0.1 eq.25
  21.9 0.1 copy.16
  22.0 0.1 mul.68
  22.2 18.0 %reduce-window.6 = s32[64,8,128]{2,1,0:T(8,128)S(1)} reduce-window(s32[64,8,128]{2,1,0:T(8,128)S(1)} %fusion.25, s32[]{:T(128)} %constant.19.clone.1), window={size=1x1x128 pad=0_0x0_0x127_0}, to_apply=%region_1.2 | reduce-window | flops 8323072 | bytes 524292 | tf_op jit(solution)/shard_map/reduce-window
  40.2 0.1 slice.18
  40.3 0.1 copy.19
  40.6 0.1 add_add_fusion
  40.8 4.3 scatter_custom_fusion.1
  45.2 4.3 scatter_custom_fusion
  49.5 0.1 broadcast_in_dim.54
  49.7 4.9 gather_fusion
  54.6 4.1 gather.18
  58.8 3.8 broadcast_select_fusion
  62.6 4.2 all-to-all-done
  66.8 6.4 all-to-all-start.1
  73.3 0.7 all-gather.2.cloned.1.call-update
  74.0 0.1 copy.21
  74.1 0.1 div.38
  74.2 4.6 gather_fusion.2
  78.8 0.1 mul.76
  78.9 4.9 gather_fusion.3
  83.8 4.6 reshape.140
  88.4 4.0 select_convert_fusion
  92.4 46.4 %all-to-all-done.1 = bf16[64,18,896]{2,1,0:T(8,128)(2,1)} async-done(((bf16[64,18,896]{2,1,0:T(8,128)(2,1)}), bf16[64,18,896]{2,1,0:T(8,128)(2,1)}, u32[]{:S(2)}, u32[]{:S(2)}) %all-to-all-start.1) | async-done | bytes 2064416 | tf_op jit(solution)/shard_map/all_to_all | solution.py:39
  138.8 7.6 %all-to-all-start.3 = ((bf16[64,18,896]{2,1,0:T(8,128)(2,1)}), bf16[64,18,896]{2,1,0:T(8,128)(2,1)}, u32[]{:S(2)}, u32[]{:S(2)}) async-start(bf16[64,18,896]{2,1,0:T(8,128)(2,1)} %select_convert_fusion), calls=%async_computation.3 | async-start | bytes 5505024 | tf_op jit(solution)/shard_map/all_to_all | solution.py:75
  146.4 2.9 convolution_convert_fusion.5
  149.4 14.7 %all-gather.2.cloned.1.call-done = bf16[1024,896]{1,0:T(8,128)(2,1)} async-done(((bf16[16,896]{1,0:T(8,128)(2,1)}), bf16[1024,896]{1,0:T(8,128)(2,1)}) %all-gather.2.cloned.1.call-update) | async-done | bytes 1835024 | tf_op jit(solution)/shard_map/all_gather | solution.py:50
  164.1 2.9 convolution_convert_fusion.4
  167.0 4.2 reshape.133
  171.2 5.5 convolution_convert_fusion.1
  176.6 35.5 %all-to-all-done.3 = bf16[64,18,896]{2,1,0:T(8,128)(2,1)} async-done(((bf16[64,18,896]{2,1,0:T(8,128)(2,1)}), bf16[64,18,896]{2,1,0:T(8,128)(2,1)}, u32[]{:S(2)}, u32[]{:S(2)}) %all-to-all-start.3) | async-done | bytes 2064416 | tf_op jit(solution)/shard_map/all_to_all | solution.py:75
  212.2 4.2 reshape.136
  216.3 6.2 convolution_convert_fusion
  222.6 112.0 %all-reduce.3.cloned.1.call-done = (bf16[1152,1024]{1,0:T(8,128)(2,1)}, bf16[128,1024]{1,0:T(8,128)(2,1)}, bf16[1152,1024]{1,0:T(8,128)(2,1)}, bf16[128,1024]{1,0:T(8,128)(2,1)}) async-done(((bf16[1152,1024]{1,0:T(8,128)(2,1)}, bf16[128,1024]{1,0:T(8,128)(2,1)}, bf16[1152,1024]{1,0:T(8,128)(2,1)}, bf16[128,1024]{1,0:T(8,128)(2,1)}), (bf16[1152,1024]{1,0:T(8,128)(2,1)}, bf16[128,1024]{1,0:T(8,128)(2,1)}, ...) | async-done | bytes 5242896 | tf_op jit(solution)/shard_map/psum | solution.py:55
  334.6 3.6 convolution_bitcast_fusion
  338.2 4.3 fusion.7
  342.5 1.4 copy-done.6
  343.9 3.8 convolution_convert_fusion.2
  347.7 4.2 reshape.137
  351.9 10.8 %all-to-all-start.4 = ((bf16[64,18,896]{2,1,0:T(8,128)(2,1)}), bf16[64,18,896]{2,1,0:T(8,128)(2,1)}, u32[]{:S(2)}, u32[]{:S(2)}) async-start(bf16[64,18,896]{2,1,0:T(8,128)(2,1)} %reshape.137), calls=%async_computation.4 | async-start | bytes 5505024 | tf_op jit(solution)/shard_map/all_to_all | solution.py:91
  362.7 0.3 reduce-scatter.5.cloned.1.call-start
  363.0 2.5 fusion.32
  365.6 5.0 convolution_convert_fusion.3
  370.5 2.3 reshape.134
  372.9 56.1 %all-to-all-done.4 = bf16[64,18,896]{2,1,0:T(8,128)(2,1)} async-done(((bf16[64,18,896]{2,1,0:T(8,128)(2,1)}), bf16[64,18,896]{2,1,0:T(8,128)(2,1)}, u32[]{:S(2)}, u32[]{:S(2)}) %all-to-all-start.4) | async-done | bytes 2064416 | tf_op jit(solution)/shard_map/all_to_all | solution.py:91
  429.0 6.9 %all-to-all-start.2 = ((bf16[64,18,896]{2,1,0:T(8,128)(2,1)}), bf16[64,18,896]{2,1,0:T(8,128)(2,1)}, u32[]{:S(2)}, u32[]{:S(2)}) async-start(bf16[64,18,896]{2,1,0:T(8,128)(2,1)} %reshape.134), calls=%async_computation.2 | async-start | bytes 5505024 | tf_op jit(solution)/shard_map/all_to_all | solution.py:61
  435.9 5.6 convert_bitcast_fusion.1
  441.5 4.1 convert_bitcast_fusion
  445.6 2.8 reshape.138
  448.4 5.3 gather_fusion.4
  453.8 51.3 %all-to-all-done.2 = bf16[64,18,896]{2,1,0:T(8,128)(2,1)} async-done(((bf16[64,18,896]{2,1,0:T(8,128)(2,1)}), bf16[64,18,896]{2,1,0:T(8,128)(2,1)}, u32[]{:S(2)}, u32[]{:S(2)}) %all-to-all-start.2) | async-done | bytes 2064416 | tf_op jit(solution)/shard_map/all_to_all | solution.py:61
  505.1 2.8 reshape.135
  507.9 5.3 gather_fusion.1
  513.2 2.9 convert_reduce_fusion
  516.1 1.2 fusion.8
  517.3 1.2 fusion.13
  518.5 2.7 fusion.14
  521.2 1.4 convert_element_type.125
  522.6 120.3 %reduce-scatter.5.cloned.1.call-done = f32[16,896]{1,0:T(8,128)} async-done(((f32[1024,896]{1,0:T(8,128)}), f32[16,896]{1,0:T(8,128)}) %reduce-scatter.5.cloned.1.call-update) | async-done | bytes 57360 | tf_op jit(solution)/shard_map/reduce_scatter | solution.py:108
  642.9 1.4 convert_element_type.126
  (47 shorter events, 0.5 us)
Async XLA Ops:
  7.2 164.0 %copy-start = (bf16[1,896,1024]{2,1,0:T(8,128)(2,1)S(1)}, bf16[1,896,1024]{2,1,0:T(8,128)(2,1)}, u32[]{:S(2)}) copy-start(bf16[1,896,1024]{2,1,0:T(8,128)(2,1)} %param.12) | copy-start | bytes 5505028
  7.2 14.4 %copy-start.12 = (s32[128,8]{0,1:T(8,128)S(1)}, s32[128,8]{0,1:T(8,128)}, u32[]{:S(2)}) copy-start(s32[128,8]{0,1:T(8,128)} %param.10) | copy-start | bytes 12292
  9.4 57.4 %all-to-all-start = ((bf16[64,896,16]{1,2,0:T(8,128)(2,1)}), bf16[64,896,16]{1,2,0:T(8,128)(2,1)}, u32[]{:S(2)}, u32[]{:S(2)}) async-start(bf16[64,896,16]{1,2,0:T(8,128)(2,1)} %stack.2), calls=%async_computation | async-start | bytes 3670016 | tf_op jit(solution)/shard_map/all_to_all | solution.py:48
  21.6 28.1 %copy-start.2 = (bf16[128,896]{1,0:T(8,128)(2,1)S(1)}, bf16[128,896]{1,0:T(8,128)(2,1)}, u32[]{:S(2)}) copy-start(bf16[128,896]{1,0:T(8,128)(2,1)} %param.8) | copy-start | bytes 688132
  62.6 11.3 %copy-start.13 = (s32[128,8]{0,1:T(8,128)S(1)}, s32[128,8]{0,1:T(8,128)}, u32[]{:S(2)}) copy-start(s32[128,8]{0,1:T(8,128)} %param.11) | copy-start | bytes 12292
  66.8 72.0 %all-to-all-start.1 = ((bf16[64,18,896]{2,1,0:T(8,128)(2,1)}), bf16[64,18,896]{2,1,0:T(8,128)(2,1)}, u32[]{:S(2)}, u32[]{:S(2)}) async-start(bf16[64,18,896]{2,1,0:T(8,128)(2,1)} %broadcast_select_fusion), calls=%async_computation.1 | async-start | bytes 5505024 | tf_op jit(solution)/shard_map/all_to_all | solution.py:39
  73.2 90.8 %all-gather.2.cloned.1.call-start = ((), (), s32[]{:S(2)}) async-start(), calls=%async_computation.7 | async-start | bytes 1863680 | tf_op jit(solution)/shard_map/all_gather | solution.py:50
  74.2 4.7 copy-start.3
  138.8 73.3 %all-to-all-start.3 = ((bf16[64,18,896]{2,1,0:T(8,128)(2,1)}), bf16[64,18,896]{2,1,0:T(8,128)(2,1)}, u32[]{:S(2)}, u32[]{:S(2)}) async-start(bf16[64,18,896]{2,1,0:T(8,128)(2,1)} %select_convert_fusion), calls=%async_computation.3 | async-start | bytes 5505024 | tf_op jit(solution)/shard_map/all_to_all | solution.py:75
  146.4 188.2 %all-reduce.3.cloned.1.call-start = ((), (), s32[]{:S(2)}) async-start(), calls=%async_computation.10 | async-start | bytes 10485760 | tf_op jit(solution)/shard_map/psum | solution.py:55
  222.5 298.7 %reduce-scatter.3.cloned.1.call-start = ((), (), s32[]{:S(2)}) async-start(), calls=%async_computation.8 | async-start | bytes 3727360 | tf_op jit(solution)/shard_map/reduce_scatter | solution.py:107
  342.5 1.4 copy-start.6
  351.9 11.1 %copy-start.10 = (bf16[128,1024]{1,0:T(8,128)(2,1)S(1)}, bf16[128,1024]{1,0:T(8,128)(2,1)}, u32[]{:S(2)}) copy-start(bf16[128,1024]{1,0:T(8,128)(2,1)} %get-tuple-element.7) | copy-start | bytes 786436
  351.9 77.0 %all-to-all-start.4 = ((bf16[64,18,896]{2,1,0:T(8,128)(2,1)}), bf16[64,18,896]{2,1,0:T(8,128)(2,1)}, u32[]{:S(2)}, u32[]{:S(2)}) async-start(bf16[64,18,896]{2,1,0:T(8,128)(2,1)} %reshape.137), calls=%async_computation.4 | async-start | bytes 5505024 | tf_op jit(solution)/shard_map/all_to_all | solution.py:91
  362.7 280.2 %reduce-scatter.5.cloned.1.call-start = ((), (), s32[]{:S(2)}) async-start(), calls=%async_computation.9 | async-start | bytes 3727360 | tf_op jit(solution)/shard_map/reduce_scatter | solution.py:108
  372.9 63.0 %copy-start.7 = (bf16[1152,896]{1,0:T(8,128)(2,1)S(1)}, bf16[1152,896]{1,0:T(8,128)(2,1)}, u32[]{:S(2)}) copy-start(bf16[1152,896]{1,0:T(8,128)(2,1)} %reshape.133) | copy-start | bytes 6193156
  429.0 76.1 %all-to-all-start.2 = ((bf16[64,18,896]{2,1,0:T(8,128)(2,1)}), bf16[64,18,896]{2,1,0:T(8,128)(2,1)}, u32[]{:S(2)}, u32[]{:S(2)}) async-start(bf16[64,18,896]{2,1,0:T(8,128)(2,1)} %reshape.134), calls=%async_computation.2 | async-start | bytes 5505024 | tf_op jit(solution)/shard_map/all_to_all | solution.py:61
  435.9 5.7 copy-start.5
  435.9 5.6 copy-start.8
  513.2 2.9 copy-start.4
  513.2 4.1 copy-start.9
  517.3 1.2 copy-start.11
  517.3 127.1 %copy-start.1 = (bf16[1,896,1024]{2,1,0:T(8,128)(2,1)S(1)}, bf16[1,896,1024]{2,1,0:T(8,128)(2,1)}, u32[]{:S(2)}) copy-start(bf16[1,896,1024]{2,1,0:T(8,128)(2,1)} %param.12) | copy-start | bytes 5505028
Sparse Core Ops, SparseCore 0:
  76.7 87.2 all-gather.1
  222.7 111.8 all-reduce.2
  338.8 158.1 reduce-scatter.2
  501.5 141.3 reduce-scatter.4
